TPU v7x, 128 devices: a whole 4x4x4 slice. The times are simulated.
128 devices in a mesh: sub: 2 (over x_hi), row: 8 (over z, x_lo), col: 8 (over y, core).
Axes of the slice: x: 4 (x_hi: 2, x_lo: 2; x = x_hi * 2 + x_lo), y: 4, z: 4, core: 2. Of those that a mesh axis runs over, the one named last changes fastest.
Arguments:
- pivot_panel: float32 [2, 1024, 1024], P('sub', 'row', 'col'), may hold values from -8 to 100, as said below
- border_panel: float32 [2, 16384, 1024], P('sub', 'row', 'col'), may hold values from -6 to 6
- window: float32 [2, 10240, 16384], P('sub', 'row', 'col'), may hold values from -6 to 6
- assembly_map: int32 [2, 10240], P('sub', 'row'), may hold values from 0 to 10239, as said below
Outputs:
- pivot_factor: float32 [2, 1024, 1024], P('sub', 'row', 'col')
- border_factor: float32 [2, 16384, 1024], P('sub', 'row', 'col')
- parent: float32 [10240, 16384], P(('sub', 'row'), 'col')
Inputs may be any that keep to these rules, and one draw needn't show every extreme that they name: `assembly_map`: for each front the map is a permutation of the parent rows; the 1280 rows of one device block send exactly 80 rows to each block of 640 parent rows. `pivot_panel`: each front's block is symmetric, and its diagonal entry exceeds 1.25 times the sum of magnitudes of the other entries of its row.
All inputs are finite; a program needn't handle non-finite values.
Results may differ from a plain program's by a relative error of at most 0.0001.
Values sent between devices are 32-bit elements; how exact they have to be, the bound alone decides.
A program may use at most 192 MiB of HBM per device.

v0:
```python
import jax
import jax.numpy as jnp
from jax import lax
from jax.sharding import PartitionSpec as P


def broadcast(value, axis, source):
    kept = jnp.where(lax.axis_index(axis) == source, value, 0).astype(value.dtype)
    return lax.psum(kept, axis)


def solve_rows(lower_diag, rows):
    return jax.scipy.linalg.solve_triangular(lower_diag, rows.T, lower=True).T


def per_device(pivot_panel, border_panel, window, assembly_map):
    row_index = lax.axis_index("row")
    col_index = lax.axis_index("col")
    pivot_local = pivot_panel[0]
    border_local = border_panel[0]
    block_rows = pivot_local.shape[0]
    col_width = pivot_local.shape[1]
    diag_piece = lax.all_gather(pivot_local, "row", axis=0, tiled=True)
    diag_block = lax.all_gather(diag_piece, "col", axis=1, tiled=True)
    lower_diag = jnp.linalg.cholesky(diag_block)
    border_full = lax.all_gather(border_local, "col", axis=1, tiled=True)
    border_lower = solve_rows(lower_diag, border_full)
    diag_rows_own = lax.dynamic_slice_in_dim(lower_diag, row_index * block_rows, block_rows, 0)
    pivot_factor = lax.dynamic_slice_in_dim(diag_rows_own, col_index * col_width, col_width, 1)
    border_factor = lax.dynamic_slice_in_dim(border_lower, col_index * col_width, col_width, 1)
    column_lower = broadcast(border_lower, "row", col_index)
    rows_kept = window.shape[1]
    product = lax.dot_general(
        border_lower[:rows_kept],
        column_lower,
        (((1,), (1,)), ((), ())),
        precision=lax.Precision.HIGHEST,
        preferred_element_type=jnp.float32,
    )
    updated = window[0] - product
    columns = updated.shape[1]
    groups = lax.axis_size("sub") * lax.axis_size("row")
    parent_rows = rows_kept // lax.axis_size("sub")
    capacity = rows_kept // groups
    target_map = assembly_map[0]
    target_group = target_map // parent_rows
    target_slot = target_map % parent_rows
    ordering = jnp.argsort(target_group, stable=True)
    send_rows = updated[ordering]
    send_slots = target_slot[ordering]
    recv_rows, recv_slots = (
        lax.all_to_all(
            send_rows.reshape(groups, capacity, columns),
            ("sub", "row"),
            split_axis=0,
            concat_axis=0,
            tiled=True,
        ),
        lax.all_to_all(
            send_slots.reshape(groups, capacity),
            ("sub", "row"),
            split_axis=0,
            concat_axis=0,
            tiled=True,
        ),
    )
    parent = (
        jnp.zeros((parent_rows, columns), jnp.float32)
        .at[recv_slots.reshape(-1)]
        .add(recv_rows.reshape(-1, columns))
    )
    return (pivot_factor[None], border_factor[None], parent)


def solution(mesh):
    in_specs = (
        P("sub", "row", "col"),
        P("sub", "row", "col"),
        P("sub", "row", "col"),
        P("sub", "row"),
    )
    out_specs = (P("sub", "row", "col"), P("sub", "row", "col"), P(("sub", "row"), "col"))
    return jax.shard_map(
        per_device, mesh=mesh, in_specs=in_specs, out_specs=out_specs, check_vma=False
    )
```

profile of v0, /device:TPU:2, one launch (start us, length us, event | category | flops | bytes accessed | tf_op | source)
XLA Modules:
  0.0 1096.8 jit_solution(15168445148168753159)
XLA Ops:
  8.1 33.3 %all-gather = f32[1,1024,128]{1,2,0:T(8,128)} all-gather(f32[1,128,128]{1,2,0:T(8,128)S(1)} %copy.10), channel_id=2, replica_groups=mesh['sub'=2,'row'=8,'col'=8] {'row'}, dimensions={1}, use_global_device_ids=true | all-gather | bytes 589824 | tf_op jit(solution)/shard_map/all_gather | solution.py:23
  42.3 32.3 %all-gather.6.cloned.1.call-done = f32[1,1024,1024]{1,2,0:T(8,128)} async-done(((f32[1,1024,128]{1,2,0:T(8,128)}), f32[1,1024,1024]{1,2,0:T(8,128)}) %all-gather.6.cloned.1.call-update) | async-done | bytes 4194320 | tf_op jit(solution)/shard_map/all_gather | solution.py:24
  74.5 5.3 copy.11
  79.9 4.4 fusion.9
  86.3 11.7 %cholesky.223 = f32[128,128]{1,0:T(8,128)S(1)} custom-call(f32[128,128]{1,0:T(8,128)S(1)} %cholesky.580), custom_call_target="Cholesky" | custom-call | tf_op jit(solution)/shard_map/jit(cholesky)/cholesky | solution.py:25
  98.0 2.5 cholesky.255
  100.6 9.8 custom-call.63
  110.4 2.3 constant_dynamic-update-slice_fusion.31
  114.3 12.2 %cholesky.244 = f32[128,128]{1,0:T(8,128)S(1)} custom-call(f32[128,128]{1,0:T(8,128)S(1)} %cholesky.584), custom_call_target="Cholesky" | custom-call | tf_op jit(solution)/shard_map/jit(cholesky)/cholesky | solution.py:25
  127.1 9.8 custom-call.64
  140.2 11.7 %cholesky.468 = f32[128,128]{1,0:T(8,128)S(1)} custom-call(f32[128,128]{1,0:T(8,128)S(1)} %cholesky.589), custom_call_target="Cholesky" | custom-call | tf_op jit(solution)/shard_map/jit(cholesky)/cholesky | solution.py:25
  152.5 9.8 custom-call.65
  163.5 2.3 convolution_subtract_fusion.7
  165.9 11.9 %cholesky.487 = f32[128,128]{1,0:T(8,128)S(1)} custom-call(f32[128,128]{1,0:T(8,128)S(1)} %cholesky.594), custom_call_target="Cholesky" | custom-call | tf_op jit(solution)/shard_map/jit(cholesky)/cholesky | solution.py:25
  178.4 9.8 custom-call.66
  189.2 2.3 convolution_subtract_fusion.8
  191.6 11.7 %cholesky.506 = f32[128,128]{1,0:T(8,128)S(1)} custom-call(f32[128,128]{1,0:T(8,128)S(1)} %cholesky.599), custom_call_target="Cholesky" | custom-call | tf_op jit(solution)/shard_map/jit(cholesky)/cholesky | solution.py:25
  203.9 10.0 custom-call.67
  217.2 11.7 %cholesky.526 = f32[128,128]{1,0:T(8,128)S(1)} custom-call(f32[128,128]{1,0:T(8,128)S(1)} %cholesky.604), custom_call_target="Cholesky" | custom-call | tf_op jit(solution)/shard_map/jit(cholesky)/cholesky | solution.py:25
  229.6 9.8 custom-call.68
  242.4 11.7 %cholesky.546 = f32[128,128]{1,0:T(8,128)S(1)} custom-call(f32[128,128]{1,0:T(8,128)S(1)} %cholesky.609), custom_call_target="Cholesky" | custom-call | tf_op jit(solution)/shard_map/jit(cholesky)/cholesky | solution.py:25
  254.7 9.8 custom-call.69
  267.2 11.7 %cholesky.564 = f32[128,128]{1,0:T(8,128)S(1)} custom-call(f32[128,128]{1,0:T(8,128)S(1)} %convolution_subtract_fusion.11), custom_call_target="Cholesky" | custom-call | tf_op jit(solution)/shard_map/jit(cholesky)/cholesky | solution.py:25
  289.2 6.8 fusion.10
  296.0 23.2 %while.1 = (s32[]{:T(128)}, f32[1024,1024]{1,0:T(8,128)}, s32[8,2]{0,1:T(2,128)S(1)}, f32[8,128,128]{2,1,0:T(8,128)S(1)}, s32[]{:T(128)}) while((s32[]{:T(128)}, f32[1024,1024]{1,0:T(8,128)}, s32[8,2]{0,1:T(2,128)S(1)}, f32[8,128,128]{2,1,0:T(8,128)S(1)}, s32[]{:T(128)}) %tuple.66), condition=%wide.while_cond, body=%wide.while_body.sunk | while | flops 2 | bytes 131189 | solution.py:13
  296.6 2.3 bitcast_dynamic-update-slice_fusion.2
  299.5 2.3 bitcast_dynamic-update-slice_fusion.2
  319.2 78.8 %custom-call.70 = f32[8,128,128]{1,2,0:T(8,128)S(1)} custom-call(f32[8,128,128]{2,1,0:T(8,128)S(1)} %get-tuple-element.12), custom_call_target="InvertDiagBlocksLowerTriangular" | custom-call | tf_op jit(solution)/shard_map/jit(_solve_triangular)/triangular_solve | solution.py:13
  398.0 2.6 constant_dynamic-update-slice_fusion.17
  400.7 3.2 convolution_subtract_fusion.4
  405.2 4.4 convolution_subtract_fusion.3
  410.9 6.5 fusion.19
  419.7 9.0 fusion.22
  428.8 2.4 constant_dynamic-update-slice_fusion.13
  431.2 10.2 convolution_subtract_fusion.2
  442.5 11.1 %convolution_subtract_fusion = f32[128,2048]{0,1:T(8,128)S(1)} fusion(f32[768,2048]{1,0:T(8,128)S(1)} %get-tuple-element.37, f32[1024,2048]{0,1:T(8,128)S(1)} %bitcast.130, f32[1024,1024]{1,0:T(8,128)} %get-tuple-element.142), kind=kOutput, calls=%fused_computation.30 | convolution fusion | flops 2416181248 | bytes 8781824 | tf_op jit(solution)/shard_map/jit(_solve_triangular)/triangular_solve | solution.py:13
  454.7 13.2 %convolution_subtract_fusion.1 = f32[128,2048]{0,1:T(8,128)S(1)} fusion(f32[896,2048]{1,0:T(8,128)S(1)} %get-tuple-element.33, f32[1024,2048]{0,1:T(8,128)S(1)} %bitcast.131, f32[1024,1024]{1,0:T(8,128)} %get-tuple-element.142), kind=kOutput, calls=%fused_computation.32 | convolution fusion | flops 2818834432 | bytes 9895936 | tf_op jit(solution)/shard_map/jit(_solve_triangular)/triangular_solve | solution.py:13
  469.1 3.3 copy-done
  472.3 4.1 broadcast_select_fusion
  477.2 5.0 sort.17
  482.3 7.1 gather_fusion
  490.0 7.9 all-to-all-start
  497.9 318.2 %all-reduce.3.cloned.1.call-done = f32[2048,1024]{0,1:T(8,128)} async-done(((f32[2048,1024]{0,1:T(8,128)}), f32[2048,1024]{0,1:T(8,128)}) %all-reduce.3.cloned.1.call-update) | async-done | bytes 8388624 | tf_op jit(solution)/shard_map/psum | solution.py:9
  816.1 39.1 %bitcast_subtract_fusion = f32[1280,2048]{1,0:T(8,128)} fusion(f32[1,1280,2048]{2,1,0:T(8,128)} %param.6, f32[2048,1024]{0,1:T(8,128)} %all-reduce.3.cloned.1.call-done, f32[2048,1024]{0,1:T(8,128)} %bitcast.121), kind=kOutput, calls=%fused_computation.5 | convolution fusion | flops 32214876160 | bytes 34603008 | tf_op jit(solution)/shard_map/dot_general | solution.py:33
  855.2 14.8 %gather_fusion.1 = f32[1280,2048]{1,0:T(8,128)} fusion(f32[1280,2048]{1,0:T(8,128)} %bitcast_subtract_fusion, s32[2048]{0:T(1024)S(1)} %pad_clamp_fusion), kind=kCustom, calls=%fused_computation.1 | custom fusion | bytes 20976640 | tf_op jit(solution)/shard_map/gather | solution.py:49
  870.0 7.4 all-to-all-start.1
  883.0 183.5 %all-to-all-done.1 = f32[16,80,2048]{2,1,0:T(8,128)} async-done(((f32[16,80,2048]{2,1,0:T(8,128)}), f32[16,80,2048]{2,1,0:T(8,128)}, u32[]{:S(2)}, u32[]{:S(2)}) %all-to-all-start.1) | async-done | bytes 10485792 | tf_op jit(solution)/shard_map/all_to_all | solution.py:52
  1066.5 23.6 %scatter_custom_fusion = f32[640,2048]{1,0:T(8,128)} fusion(s32[1280]{0:T(1024)S(1)} %fusion.70, f32[1280,2048]{1,0:T(8,128)} %bitcast.33, f32[]{:T(128)} %constant.306.clone.1), kind=kCustom, calls=%fused_computation.27 | custom fusion | flops 2621440 | bytes 5243392 | tf_op jit(solution)/shard_map/scatter-add | solution.py:70
  (97 shorter events, 62.3 us)
Async XLA Ops:
  7.2 67.4 %all-gather.6.cloned.1.call-start = ((), (), s32[]{:S(2)}) async-start(), calls=%async_computation.3 | async-start | bytes 4718592 | tf_op jit(solution)/shard_map/all_gather | solution.py:24
  41.4 356.5 %all-gather.8.cloned.1.call-start = ((), (), s32[]{:S(2)}) async-start(), calls=%async_computation.4 | async-start | bytes 9437184 | tf_op jit(solution)/shard_map/all_gather | solution.py:26
  42.2 773.9 %all-reduce.3.cloned.1.call-start = ((), (), s32[]{:S(2)}) async-start(), calls=%async_computation.2 | async-start | bytes 16777216 | tf_op jit(solution)/shard_map/psum | solution.py:9
  84.3 2.0 copy-start.1
  398.0 7.2 slice-start
  400.6 4.5 slice-start.1
  469.1 3.3 copy-start
  476.4 0.7 copy-start.2
  490.0 380.0 %all-to-all-start = ((s32[16,1,80]{2,1,0:T(1,128)}), s32[16,1,80]{2,1,0:T(1,128)S(1)}, u32[]{:S(2)}, u32[]{:S(2)}) async-start(s32[16,1,80]{2,1,0:T(1,128)} %all_to_all.9), calls=%async_computation | async-start | bytes 16384 | tf_op jit(solution)/shard_map/all_to_all | solution.py:59
  870.0 196.5 %all-to-all-start.1 = ((f32[16,80,2048]{2,1,0:T(8,128)}), f32[16,80,2048]{2,1,0:T(8,128)}, u32[]{:S(2)}, u32[]{:S(2)}) async-start(f32[16,80,2048]{2,1,0:T(8,128)} %bitcast.119), calls=%async_computation.1 | async-start | bytes 20971520 | tf_op jit(solution)/shard_map/all_to_all | solution.py:52
Sparse Core Ops, SparseCore 0:
  41.6 32.9 all-gather.5
  76.2 53.4 all-gather.7
  476.6 339.5 all-reduce.2
where the time goes:
time: 1110 us; the launch traced here: 1100 us
  waiting for transfers between devices  535 us (48%)
  other arithmetic  296 us (27%)
  matrix products  133 us (12%)
  local copies, waits for them, and re-layouts  65.2 us (6%)
  blocking collectives  33.3 us (3%)
  between operations  19.6 us (2%)
  starting transfers between devices  15.5 us (1%)
    psum x1, waiting for transfers between devices, broadcast(): return lax.psum(kept, axis)  318 us
    all_to_all x1, waiting for transfers between devices, per_device(): lax.all_to_all(send_rows.reshape(groups, capacity, columns), ('sub', 'row...  183 us
    another operation x30, other arithmetic, per_device(): lower_diag = jnp.linalg.cholesky(diag_block)  172 us
    another operation x3, other arithmetic, solve_rows(): return jax.scipy.linalg.solve_triangular(lower_diag, rows.T, lower=True).T  85.6 us
    another operation x15, matrix products, solve_rows(): return jax.scipy.linalg.solve_triangular(lower_diag, rows.T, lower=True).T  70.9 us
    dot_general x1, matrix products, per_device(): lax.dot_general(border_lower[:rows_kept], column_lower, (((1,), (1,)), ((...  39.1 us
    all_gather x1, blocking collectives, per_device(): diag_piece = lax.all_gather(pivot_local, 'row', axis=0, tiled=True)  33.3 us
    all_gather x1, waiting for transfers between devices, per_device(): diag_block = lax.all_gather(diag_piece, 'col', axis=1, tiled=True)  32.3 us
  transfers between devices with their start and end apart: 5, of which 3 were waited for; matrix products, arithmetic and copies ran while one was open for 35% of the time, Pallas kernels for 0%

commit v1 on v0

v1 whole, which is shorter than its diff:
```python
import functools

import jax
import jax.numpy as jnp
from jax import lax
from jax.experimental import pallas as pl
from jax.experimental.pallas import tpu as pltpu
from jax.sharding import PartitionSpec as P

NB = 128
F32 = jnp.float32
BF16 = jnp.bfloat16


def split(x):
    hi = x.astype(BF16)
    return hi, (x - hi.astype(F32)).astype(BF16)


def dot_nn(a, b):
    return lax.dot_general(a, b, (((1,), (0,)), ((), ())), preferred_element_type=F32)


def dot_nt(a, b):
    return lax.dot_general(a, b, (((1,), (1,)), ((), ())), preferred_element_type=F32)


def dot3_nn(a_hi, a_lo, b_hi, b_lo):
    return dot_nn(jnp.concatenate([a_hi, a_lo, a_hi], axis=1), jnp.concatenate([b_hi, b_hi, b_lo], axis=0))


def dot3_nt(a_hi, a_lo, b_hi, b_lo):
    return dot_nt(jnp.concatenate([a_hi, a_lo, a_hi], axis=1), jnp.concatenate([b_hi, b_hi, b_lo], axis=1))


def eliminate(blocks):
    lane = lax.broadcasted_iota(jnp.int32, (8, NB), 1)
    sub = lax.broadcasted_iota(jnp.int32, (8, NB), 0)
    for j in range(NB):
        g, r = divmod(j, 8)
        at_j = lane == j
        for block in blocks:
            row = jnp.broadcast_to(block[g][r : r + 1, :], (8, NB))
            pivot = jnp.broadcast_to(row[:, j : j + 1], (8, NB))
            inv = 1.0 / pivot
            scaled = jnp.where(at_j, inv, row * inv)
            for i in range(g, NB // 8):
                column = jnp.broadcast_to(block[i][:, j : j + 1], (8, NB))
                kept = jnp.where(at_j, 0.0, block[i])
                new = kept - column * scaled
                if i == g:
                    new = jnp.where(sub > r, new, block[i])
                block[i] = new
    return blocks


def factor_kernel(where_ref, pivot_ref, hi_ref, lo_ref, factor_ref, work, panel):
    fronts = work.shape[0]
    size = work.shape[1]
    steps = size // NB
    own, row_at, col_at = where_ref[0], where_ref[1], where_ref[2]
    for f in range(fronts):
        for r in range(steps):
            for c in range(steps):
                work[f, r * NB : (r + 1) * NB, c * NB : (c + 1) * NB] = pivot_ref[(f * steps + r) * steps + c]
    lane = lax.broadcasted_iota(jnp.int32, (NB, NB), 1)
    sub = lax.broadcasted_iota(jnp.int32, (NB, NB), 0)
    factor_ref[...] = jnp.zeros_like(factor_ref)

    def step(j, carry):
        base = pl.multiple_of(j * NB, NB)
        here = pl.ds(base, NB)
        blocks = []
        for f in range(fronts):
            blocks.append([work[f, pl.ds(base + 8 * i, 8), here] for i in range(NB // 8)])
        blocks = eliminate(blocks)
        columns = lax.broadcasted_iota(jnp.int32, (NB, size), 1)
        rows = lax.broadcasted_iota(jnp.int32, (size, NB), 0)
        for f in range(fronts):
            done = jnp.concatenate(blocks[f], axis=0)
            diag = jnp.sum(jnp.where(lane == sub, done, 0.0), axis=1, keepdims=True)
            scale = lax.rsqrt(diag)
            inverse = jnp.where(lane < sub, done, jnp.where(lane == sub, 1.0, 0.0)) * scale
            upper = jnp.where(lane >= sub, done, 0.0) * scale
            inv_hi, inv_lo = split(inverse)
            below_hi, below_lo = split(work[f, :, here])
            left = dot3_nt(below_hi, below_lo, inv_hi, inv_lo)
            left = jnp.where(rows >= base + NB, left, 0.0)
            panel[f] = left
            work[f, here, here] = jnp.zeros((NB, NB), F32)
            right_hi, right_lo = split(work[f, here, :])
            right = dot3_nn(inv_hi, inv_lo, right_hi, right_lo)
            work[f, here, :] = right
            work[f, here, here] = inverse
            full = work[f, here, :]
            lower = jnp.where(columns < base + NB, full, 0.0)
            low_hi, low_lo = split(lower)
            hi_ref[f, here, :] = low_hi
            lo_ref[f, here, :] = low_lo
            full_hi, full_lo = split(full)
            stacked = jnp.concatenate([full_hi, full_hi, full_lo], axis=0)

            @pl.when(jnp.logical_and(j == col_at, own == f))
            def _():
                factor_ref[...] = jnp.where(
                    row_at == j, upper.T, panel[f, pl.ds(pl.multiple_of(row_at * NB, NB), NB), :]
                )

            def trail(i, carry):
                at = pl.ds(pl.multiple_of(i * NB, NB), NB)
                work[f, at, here] = jnp.zeros((NB, NB), F32)
                l_hi, l_lo = split(panel[f, at, :])
                work[f, at, :] -= dot_nn(jnp.concatenate([l_hi, l_lo, l_hi], axis=1), stacked)
                return carry

            lax.fori_loop(j + 1, steps, trail, 0)
        return carry

    lax.fori_loop(0, steps, step, 0)


def factor_fronts(where, pivots, fronts, size):
    return pl.pallas_call(
        factor_kernel,
        in_specs=[pl.BlockSpec(memory_space=pltpu.SMEM), pl.BlockSpec(memory_space=pltpu.VMEM)],
        out_specs=[pl.BlockSpec(memory_space=pltpu.VMEM)] * 3,
        out_shape=[
            jax.ShapeDtypeStruct((fronts, size, size), BF16),
            jax.ShapeDtypeStruct((fronts, size, size), BF16),
            jax.ShapeDtypeStruct((NB, NB), F32),
        ],
        scratch_shapes=[pltpu.VMEM((fronts, size, size), F32), pltpu.VMEM((fronts, size, NB), F32)],
        compiler_params=pltpu.CompilerParams(vmem_limit_bytes=60 << 20),
        name="factor_fronts",
        cost_estimate=pl.CostEstimate(flops=20_000_000_000, bytes_accessed=16 << 20, transcendentals=0),
    )(where, pivots)


def rows_kernel(rows_ref, inv_hi_ref, inv_lo_ref, hi_ref, lo_ref):
    size = inv_hi_ref.shape[1]
    wide = 256
    raw = jnp.concatenate([rows_ref[k] for k in range(rows_ref.shape[0])], axis=1)
    raw_hi, raw_lo = split(raw)
    solved = []
    for n in range(0, size, wide):
        part = slice(0, n + wide)
        at = slice(n, n + wide)
        solved.append(
            dot3_nt(raw_hi[:, part], raw_lo[:, part], inv_hi_ref[0, at, part], inv_lo_ref[0, at, part])
        )
    solved_hi, solved_lo = split(jnp.concatenate(solved, axis=1))
    for n in range(0, size, wide):
        at = slice(n, n + wide)
        out = dot3_nn(solved_hi[:, n:], solved_lo[:, n:], inv_hi_ref[0, n:, at], inv_lo_ref[0, n:, at])
        hi_ref[0, :, at], lo_ref[0, :, at] = split(out)


def solve_both(rows, inv_hi, inv_lo, tile=320):
    steps, total, _ = rows.shape
    fronts, size, _ = inv_hi.shape
    per = total // fronts
    inv_spec = pl.BlockSpec((1, size, size), lambda f, i: (f, 0, 0))
    out_spec = pl.BlockSpec((1, tile, size), lambda f, i: (f, i, 0))
    return pl.pallas_call(
        rows_kernel,
        grid=(fronts, per // tile),
        in_specs=[pl.BlockSpec((steps, tile, NB), lambda f, i: (0, f * (per // tile) + i, 0)), inv_spec, inv_spec],
        out_specs=[out_spec, out_spec],
        out_shape=[jax.ShapeDtypeStruct((fronts, per, size), BF16)] * 2,
        compiler_params=pltpu.CompilerParams(vmem_limit_bytes=60 << 20),
        name="solve_both",
        cost_estimate=pl.CostEstimate(flops=12_000_000_000, bytes_accessed=18 << 20, transcendentals=0),
    )(rows, inv_hi, inv_lo)


def border_kernel(where_ref, raw_ref, hi_ref, lo_ref, out_ref):
    raw_hi, raw_lo = split(jnp.concatenate([raw_ref[k] for k in range(raw_ref.shape[0])], axis=1))
    out_ref[...] = dot3_nt(raw_hi, raw_lo, hi_ref[0], lo_ref[0])


def solve_border(where, columns, inv_hi, inv_lo, tile=512):
    fronts, size, _ = inv_hi.shape
    steps = size // NB
    rows = columns.shape[1]
    inv_spec = pl.BlockSpec((1, NB, size), lambda i, w: (w[0], w[1], 0))
    return pl.pallas_call(
        border_kernel,
        grid_spec=pltpu.PrefetchScalarGridSpec(
            num_scalar_prefetch=1,
            grid=(rows // tile,),
            in_specs=[pl.BlockSpec((steps, tile, NB), lambda i, w: (w[0], i, 0)), inv_spec, inv_spec],
            out_specs=pl.BlockSpec((tile, NB), lambda i, w: (i, 0)),
        ),
        out_shape=jax.ShapeDtypeStruct((rows, NB), F32),
        compiler_params=pltpu.CompilerParams(vmem_limit_bytes=60 << 20),
        name="solve_border",
        cost_estimate=pl.CostEstimate(flops=1_600_000_000, bytes_accessed=10 << 20, transcendentals=0),
    )(where, columns, inv_hi, inv_lo)


def product_kernel(hi_ref, lo_ref, columns_ref, out_ref):
    fronts = hi_ref.shape[0]
    steps = columns_ref.shape[0] // fronts
    total = None
    for f in range(fronts):
        raw = jnp.concatenate([columns_ref[f * steps + k] for k in range(steps)], axis=1)
        c_hi, c_lo = split(raw)
        part = dot3_nt(hi_ref[f], lo_ref[f], c_hi, c_lo)
        total = part if total is None else total + part
    out_ref[...] = total


def product(rows_hi, rows_lo, columns, tile=256):
    fronts, per, size = rows_hi.shape
    blocks, width, _ = columns.shape
    rows_spec = pl.BlockSpec((fronts, per, size), lambda i: (0, 0, 0), pipeline_mode=pl.Buffered(1))
    return pl.pallas_call(
        product_kernel,
        grid=(width // tile,),
        in_specs=[rows_spec, rows_spec, pl.BlockSpec((blocks, tile, NB), lambda i: (0, i, 0))],
        out_specs=pl.BlockSpec((per, tile), lambda i: (0, i)),
        out_shape=jax.ShapeDtypeStruct((per, width), F32),
        compiler_params=pltpu.CompilerParams(vmem_limit_bytes=60 << 20),
        name="product",
        cost_estimate=pl.CostEstimate(flops=16_000_000_000, bytes_accessed=27 << 20, transcendentals=0),
    )(rows_hi, rows_lo, columns)


def assemble_kernel(place_ref, arrived_ref, product_ref, out_ref):
    per = out_ref.shape[0]

    def group(s, carry):
        base = pl.multiple_of(s * 8, 8)
        picked = []
        for r in range(8):
            first = arrived_ref[pl.ds(place_ref[base + r], 1), :]
            second = arrived_ref[pl.ds(place_ref[per + base + r], 1), :]
            picked.append(first + second)
        out_ref[pl.ds(base, 8), :] = jnp.concatenate(picked, axis=0) - product_ref[pl.ds(base, 8), :]
        return carry

    lax.fori_loop(0, per // 8, group, 0)


def assemble(place, arrived, products, tile=256):
    total, width = arrived.shape
    per = products.shape[0]
    return pl.pallas_call(
        assemble_kernel,
        grid_spec=pltpu.PrefetchScalarGridSpec(
            num_scalar_prefetch=1,
            grid=(width // tile,),
            in_specs=[
                pl.BlockSpec((total, tile), lambda i, w: (0, i)),
                pl.BlockSpec((per, tile), lambda i, w: (0, i)),
            ],
            out_specs=pl.BlockSpec((per, tile), lambda i, w: (0, i)),
        ),
        out_shape=jax.ShapeDtypeStruct((per, width), F32),
        compiler_params=pltpu.CompilerParams(vmem_limit_bytes=60 << 20),
        name="assemble",
        cost_estimate=pl.CostEstimate(flops=4_000_000, bytes_accessed=21 << 20, transcendentals=0),
    )(place, arrived, products)


def per_device(pivot_panel, border_panel, window, assembly_map):
    front = lax.axis_index("sub")
    row_index = lax.axis_index("row")
    col_index = lax.axis_index("col")
    fronts, n_row, n_col = lax.axis_size("sub"), lax.axis_size("row"), lax.axis_size("col")
    pivot_local, border_local, window_local = pivot_panel[0], border_panel[0], window[0]
    size = n_row * pivot_local.shape[0]
    rows_kept, width = window_local.shape
    groups = fronts * n_row
    per = rows_kept // fronts
    capacity = rows_kept // groups
    both = ("sub", "row")
    turn = [(r * n_col + c, c * n_row + r) for r in range(n_row) for c in range(n_col)]

    targets, ordering = lax.sort((assembly_map[0], lax.iota(jnp.int32, rows_kept)), num_keys=1)

    def exchange(x):
        return lax.all_to_all(x, both, split_axis=0, concat_axis=0, tiled=True)

    pivots = lax.all_gather(pivot_local, ("sub", "row", "col"), axis=0)
    columns = lax.ppermute(border_local, ("row", "col"), turn)
    columns = lax.all_gather(columns, both, axis=0)
    slots = exchange((targets % per).reshape(groups, capacity)).reshape(-1)
    arrived_rows = exchange(border_local[:rows_kept][ordering].reshape(groups, capacity, NB)).reshape(rows_kept, NB)
    arrived = exchange(window_local[ordering].reshape(groups, capacity, width)).reshape(rows_kept, width)
    owner = lax.iota(jnp.int32, rows_kept) // per
    _, place = lax.sort((slots + owner * per, lax.iota(jnp.int32, rows_kept)), num_keys=1)
    rows = lax.all_gather(arrived_rows[place], "col", axis=0)

    where = jnp.stack([front, row_index, col_index])
    inv_hi, inv_lo, pivot_factor = factor_fronts(where, pivots, fronts, size)
    turned = solve_border(where, columns, inv_hi, inv_lo)
    border_factor = lax.ppermute(turned, ("row", "col"), turn)
    rows_hi, rows_lo = solve_both(rows, inv_hi, inv_lo)
    products = product(rows_hi, rows_lo, columns)
    parent = assemble(place, arrived, products)
    return (pivot_factor[None], border_factor[None], parent)


def solution(mesh):
    in_specs = (
        P("sub", "row", "col"),
        P("sub", "row", "col"),
        P("sub", "row", "col"),
        P("sub", "row"),
    )
    out_specs = (P("sub", "row", "col"), P("sub", "row", "col"), P(("sub", "row"), "col"))
    return jax.shard_map(
        per_device, mesh=mesh, in_specs=in_specs, out_specs=out_specs, check_vma=False
    )
```

time: 1110 us -> 839 us (0.76)
  other arithmetic: 296 us -> 11.5 us
  Pallas kernels: 0 us -> 248 us
  matrix products: 133 us -> 0 us
  waiting for transfers between devices: 535 us -> 478 us
  starting transfers between devices: 15.5 us -> 57.4 us
  local copies, waits for them, and re-layouts: 65.2 us -> 25.3 us
  blocking collectives: 33.3 us -> 0 us
    all_gather x2 -> x3, waiting for transfers between devices: 32.3 us -> 453 us  [the longest x1 257 us: per_device(): pivots = lax.all_gather(pivot_local, ('sub', 'row', 'col'), axis=0)]
    psum x1 -> x0, waiting for transfers between devices: 318 us -> none  [broadcast(): return lax.psum(kept, axis)]
    another operation x33 -> x1, other arithmetic: 258 us -> 0.61 us  [per_device(): where = jnp.stack([front, row_index, col_index])]
    pallas_call x0 -> x5, Pallas kernels: none -> 248 us  [the longest x1 176 us: factor_fronts(): pl.pallas_call(factor_kernel, in_specs=[pl.BlockSpec(memory_space=pltpu.S...]
    all_to_all x2 -> x3, waiting for transfers between devices: 183 us -> 8.28 us  [exchange(): return lax.all_to_all(x, both, split_axis=0, concat_axis=0, tiled=True)]
    another operation x29 -> x0, matrix products: 93.8 us -> none  [the longest x15 70.9 us: solve_rows(): return jax.scipy.linalg.solve_triangular(lower_diag, rows.T, lower=True).T]
    dot_general x1 -> x0, matrix products: 39.1 us -> none  [per_device(): lax.dot_general(border_lower[:rows_kept], column_lower, (((1,), (1,)), ((...]
    all_to_all x2 -> x3, starting transfers between devices: 15.3 us -> 53.5 us  [exchange(): return lax.all_to_all(x, both, split_axis=0, concat_axis=0, tiled=True)]
  transfers between devices with their start and end apart: 5 -> 8, of which waited for: 3 -> 5; matrix products, arithmetic and copies ran while one was open for 35% -> 4% of each run, Pallas kernels for 0% -> 30%
where the time goes in v1:
time: 839 us; the launch traced here: 834 us
  waiting for transfers between devices  478 us (57%)
  Pallas kernels  248 us (30%)
  starting transfers between devices  57.4 us (7%)
  local copies, waits for them, and re-layouts  25.3 us (3%)
  between operations  13.8 us (2%)
  other arithmetic  11.5 us (1%)
    all_gather x1, waiting for transfers between devices, per_device(): pivots = lax.all_gather(pivot_local, ('sub', 'row', 'col'), axis=0)  257 us
    all_gather x1, waiting for transfers between devices, per_device(): columns = lax.all_gather(columns, both, axis=0)  196 us
    pallas_call x1, Pallas kernels, factor_fronts(): pl.pallas_call(factor_kernel, in_specs=[pl.BlockSpec(memory_space=pltpu.S...  176 us
    all_to_all x3, starting transfers between devices, exchange(): return lax.all_to_all(x, both, split_axis=0, concat_axis=0, tiled=True)  53.5 us
    pallas_call x1, Pallas kernels, assemble(): pl.pallas_call(assemble_kernel, grid_spec=pltpu.PrefetchScalarGridSpec(nu...  26.5 us
    pallas_call x1, Pallas kernels, product(): pl.pallas_call(product_kernel, grid=(width // tile,), in_specs=[rows_spec...  22.1 us
  transfers between devices with their start and end apart: 8, of which 5 were waited for; matrix products, arithmetic and copies ran while one was open for 4% of the time, Pallas kernels for 30%

profile of v1, /device:TPU:2, one launch (start us, length us, event | category | flops | bytes accessed | tf_op | source)
XLA Modules:
  0.0 834.2 jit_solution(986822799319118884)
XLA Ops:
  7.2 0.0 copy-start.1
  7.2 0.0 all-gather.6.cloned.1.call-start
  7.2 0.7 all-gather.6.cloned.1.call-update
  7.9 0.7 reduce
  8.6 4.4 sort.30
  13.1 0.7 all_to_all.12
  13.8 8.3 all-to-all-start
  22.1 1.1 slice_bitcast_fusion
  23.3 3.2 gather_fusion.1
  26.4 1.8 all-to-all-done
  28.2 5.4 all-to-all-start.2
  33.6 0.0 all-gather.10.cloned.1.call-start
  33.7 0.5 broadcast.24
  34.2 0.7 reduce.4
  34.9 0.1 reshape.27
  35.0 5.0 sort.31
  40.0 0.0 copy-start.2
  40.0 6.4 all-to-all-done.2
  46.5 3.1 gather_fusion.2
  49.6 0.0 all-gather.10.cloned.1.call-update
  49.6 0.0 all-gather.8.cloned.1.call-start
  49.7 0.0 copy-done.1
  49.7 1.9 collective-permute-start
  51.6 16.1 %collective-permute-done = f32[2048,128]{1,0:T(8,128)S(1)} collective-permute-done((f32[2048,128]{1,0:T(8,128)S(1)}, f32[2048,128]{1,0:T(8,128)S(1)}, u32[]{:S(2)}, u32[]{:S(2)}) %collective-permute-start) | collective-permute-done | bytes 1048608 | tf_op jit(solution)/shard_map/ppermute | solution.py:286
  67.7 0.0 copy-start
  67.7 1.0 copy-done
  68.7 0.0 all-gather.8.cloned.1.call-update
  68.7 14.7 %gather_fusion = f32[1280,2048]{1,0:T(8,128)} fusion(f32[1280,2048]{1,0:T(8,128)} %bitcast.15, s32[2048]{0:T(1024)S(1)} %pad_clamp_fusion.1), kind=kCustom, calls=%fused_computation | custom fusion | bytes 20976640 | tf_op jit(solution)/shard_map/gather | solution.py:290
  83.4 0.0 copy-done.2
  83.4 39.8 %all-to-all-start.1 = ((f32[16,80,2048]{2,1,0:T(8,128)}), f32[16,80,2048]{2,1,0:T(8,128)}, u32[]{:S(2)}, u32[]{:S(2)}) async-start(f32[16,80,2048]{2,1,0:T(8,128)} %bitcast.17), calls=%async_computation.1 | async-start | bytes 20971520 | tf_op jit(solution)/shard_map/all_to_all | solution.py:283
  123.2 0.6 pad_add_fusion.where_ref
  123.8 257.1 %all-gather.6.cloned.1.call-done.pivot_ref = f32[128,128,128]{2,1,0:T(8,128)} async-done(((f32[1,128,128]{2,1,0:T(8,128)}), f32[128,128,128]{2,1,0:T(8,128)}) %all-gather.6.cloned.1.call-update) | async-done | bytes 8388624 | tf_op jit(solution)/shard_map/all_gather | solution.py:285
  380.9 175.7 %factor_fronts.1 = (bf16[2,1024,1024]{2,1,0:T(8,128)(2,1)}, bf16[2,1024,1024]{2,1,0:T(8,128)(2,1)}, f32[128,128]{1,0:T(8,128)}) custom-call(s32[3]{0:T(128)} %pad_add_fusion.where_ref, f32[128,128,128]{2,1,0:T(8,128)} %all-gather.6.cloned.1.call-done.pivot_ref), custom_call_target="tpu_custom_call" | custom-call | flops 20000000000 | bytes 16777216 | tf_op jit(solution)/shard_map/factor_fronts/pallas_call | solution.py:123
  556.6 0.0 all-gather.10.cloned.1.call-done
  556.6 16.0 %solve_both.1 = (bf16[2,640,1024]{2,1,0:T(8,128)(2,1)}, bf16[2,640,1024]{2,1,0:T(8,128)(2,1)}) custom-call(f32[8,1280,128]{2,1,0:T(8,128)} %bitcast.22, bf16[2,1024,1024]{2,1,0:T(8,128)(2,1)} %get-tuple-element.12.hi_ref.inv_hi_ref, bf16[2,1024,1024]{2,1,0:T(8,128)(2,1)} %get-tuple-element.13.lo_ref.inv_lo_ref), custom_call_target="tpu_custom_call" | custom-call | flops 12000000000 | bytes 18874368 | tf_op jit(solution)/shard_map/solve_both/pallas_call | solution.py:164
  572.6 195.6 %all-gather.8.cloned.1.call-done = f32[32768,128]{1,0:T(8,128)} async-done(((f32[2048,128]{1,0:T(8,128)}), f32[32768,128]{1,0:T(8,128)}) %all-gather.8.cloned.1.call-update) | async-done | bytes 16777232 | tf_op jit(solution)/shard_map/all_gather | solution.py:287
  768.2 7.9 solve_border.1
  776.1 1.9 collective-permute-start.1
  778.1 22.1 %product.1.product_ref = f32[640,2048]{1,0:T(8,128)} custom-call(bf16[2,640,1024]{2,1,0:T(8,128)(2,1)} %get-tuple-element.17.hi_ref, bf16[2,640,1024]{2,1,0:T(8,128)(2,1)} %get-tuple-element.18.lo_ref, f32[16,2048,128]{2,1,0:T(8,128)} %bitcast.19), custom_call_target="tpu_custom_call" | custom-call | flops 16000000000 | bytes 28311552 | tf_op jit(solution)/shard_map/product/pallas_call | solution.py:217
  800.2 0.0 all-to-all-done.1
  800.2 26.5 %assemble.1 = f32[640,2048]{1,0:T(8,128)} custom-call(s32[1280]{0:T(1024)} %copy-done.2, f32[1280,2048]{1,0:T(8,128)} %bitcast.9.arrived_ref, f32[640,2048]{1,0:T(8,128)} %product.1.product_ref), custom_call_target="tpu_custom_call" | custom-call | flops 4000000 | bytes 22020096 | tf_op jit(solution)/shard_map/assemble/pallas_call | solution.py:248
  826.7 0.0 collective-permute-done.1
  826.7 1.0 copy.8
  (8 shorter events, 0.1 us)
Async XLA Ops:
  7.2 42.5 %copy-start.1 = (f32[1,2048,128]{2,1,0:T(8,128)S(1)}, f32[1,2048,128]{2,1,0:T(8,128)}, u32[]{:S(2)}) copy-start(f32[1,2048,128]{2,1,0:T(8,128)} %param.5) | copy-start | bytes 3145732
  7.2 373.8 %all-gather.6.cloned.1.call-start = ((), (), s32[]{:S(2)}) async-start(), calls=%async_computation.3 | async-start | bytes 8454144 | tf_op jit(solution)/shard_map/all_gather | solution.py:285
  13.8 14.5 %all-to-all-start = ((s32[16,1,80]{2,1,0:T(1,128)}), s32[16,1,80]{2,1,0:T(1,128)S(1)}, u32[]{:S(2)}, u32[]{:S(2)}) async-start(s32[16,1,80]{2,1,0:T(1,128)} %all_to_all.12), calls=%async_computation | async-start | bytes 16384 | tf_op jit(solution)/shard_map/all_to_all | solution.py:283
  28.2 18.2 %all-to-all-start.2 = ((f32[16,80,128]{2,1,0:T(8,128)}), f32[16,80,128]{2,1,0:T(8,128)S(1)}, u32[]{:S(2)}, u32[]{:S(2)}) async-start(f32[16,80,128]{2,1,0:T(8,128)} %bitcast.11), calls=%async_computation.2 | async-start | bytes 1310720 | tf_op jit(solution)/shard_map/all_to_all | solution.py:283
  33.6 523.0 %all-gather.10.cloned.1.call-start = ((), (), s32[]{:S(2)}) async-start(), calls=%async_computation.5 | async-start | bytes 5898240 | tf_op jit(solution)/shard_map/all_gather | solution.py:293
  40.0 43.4 %copy-start.2 = (s32[1280]{0:T(1024)}, s32[1280]{0:T(1024)S(1)}, u32[]{:S(2)}) copy-start(s32[1280]{0:T(1024)S(1)} %get-tuple-element.15.place_ref) | copy-start | bytes 15364
  49.6 718.6 %all-gather.8.cloned.1.call-start = ((), (), s32[]{:S(2)}) async-start(), calls=%async_computation.4 | async-start | bytes 17825792 | tf_op jit(solution)/shard_map/all_gather | solution.py:287
  49.7 18.0 %collective-permute-start = (f32[2048,128]{1,0:T(8,128)S(1)}, f32[2048,128]{1,0:T(8,128)S(1)}, u32[]{:S(2)}, u32[]{:S(2)}) collective-permute-start(f32[2048,128]{1,0:T(8,128)S(1)} %bitcast.21), channel_id=1, source_target_pairs={{0,0},{1,8},{2,16},{3,24},{4,32},{5,40},{6,48},{7,56},{8,1},{9,9},... | collective-permute-start | bytes 3145736 | tf_op jit(solution)/shard_map/ppermute | solution.py:286
  67.7 1.0 copy-start
  83.4 716.7 %all-to-all-start.1 = ((f32[16,80,2048]{2,1,0:T(8,128)}), f32[16,80,2048]{2,1,0:T(8,128)}, u32[]{:S(2)}, u32[]{:S(2)}) async-start(f32[16,80,2048]{2,1,0:T(8,128)} %bitcast.17), calls=%async_computation.1 | async-start | bytes 20971520 | tf_op jit(solution)/shard_map/all_to_all | solution.py:283
  776.1 50.6 %collective-permute-start.1 = (f32[2048,128]{1,0:T(8,128)}, f32[2048,128]{1,0:T(8,128)S(1)}, u32[]{:S(2)}, u32[]{:S(2)}) collective-permute-start(f32[2048,128]{1,0:T(8,128)} %solve_border.1), channel_id=1, source_target_pairs={{0,0},{1,8},{2,16},{3,24},{4,32},{5,40},{6,48},{7,56},{8,1},{9,9},... | collective-permute-start | bytes 3145736 | tf_op jit(solution)/shard_map/ppermute | solution.py:298
Sparse Core Ops, SparseCore 0:
  9.7 371.1 all-gather.5
  382.6 34.7 all-gather.9
  419.7 348.4 all-gather.7

commit v2 on v1

--- a/solution.py
+++ b/solution.py
@@ -36,21 +36,50 @@
 def eliminate(blocks):
     lane = lax.broadcasted_iota(jnp.int32, (8, NB), 1)
     sub = lax.broadcasted_iota(jnp.int32, (8, NB), 0)
-    for j in range(NB):
-        g, r = divmod(j, 8)
-        at_j = lane == j
+    shape = (8, NB)
+    for g in range(NB // 8):
+        first = 8 * g
         for block in blocks:
-            row = jnp.broadcast_to(block[g][r : r + 1, :], (8, NB))
-            pivot = jnp.broadcast_to(row[:, j : j + 1], (8, NB))
-            inv = 1.0 / pivot
-            scaled = jnp.where(at_j, inv, row * inv)
-            for i in range(g, NB // 8):
-                column = jnp.broadcast_to(block[i][:, j : j + 1], (8, NB))
-                kept = jnp.where(at_j, 0.0, block[i])
-                new = kept - column * scaled
-                if i == g:
-                    new = jnp.where(sub > r, new, block[i])
-                block[i] = new
+            rows = [jnp.broadcast_to(block[g][k : k + 1, :], shape) for k in range(8)]
+            scalar = {
+                (k, n): jnp.broadcast_to(rows[k][:, first + n : first + n + 1], shape)
+                for k in range(8)
+                for n in range(k, 8)
+            }
+            inverse, factor = [], {}
+            for k in range(8):
+                inv = 1.0 / scalar[k, k]
+                inverse.append(inv)
+                unit = jnp.where(lane == first + k, 1.0, rows[k])
+                for n in range(k + 1, 8):
+                    m = scalar[k, n] * inv
+                    factor[k, n] = m
+                    for q in range(n, 8):
+                        scalar[n, q] = scalar[n, q] - m * scalar[k, q]
+                    rows[n] = jnp.where(lane == first + k, 0.0, rows[n]) - m * unit
+            scaled = []
+            for k in range(8):
+                hat = jnp.where(lane == first + k, 1.0, rows[k])
+                if k < 7:
+                    hat = jnp.where(jnp.logical_and(lane > first + k, lane < first + 8), 0.0, hat)
+                scaled.append(hat * inverse[k])
+            for i in range(g + 1, NB // 8):
+                column = [jnp.broadcast_to(block[i][:, first + k : first + k + 1], shape) for k in range(8)]
+                for k in range(8):
+                    for n in range(k + 1, 8):
+                        column[n] = column[n] - column[k] * factor[k, n]
+                inside = jnp.logical_and(lane >= first, lane < first + 8)
+                rest = jnp.where(inside, 0.0, block[i])
+                even = column[0] * scaled[0]
+                odd = column[1] * scaled[1]
+                for k in range(2, 8, 2):
+                    even = even + column[k] * scaled[k]
+                    odd = odd + column[k + 1] * scaled[k + 1]
+                block[i] = rest - (even + odd)
+            own = rows[0]
+            for k in range(1, 8):
+                own = jnp.where(sub == k, rows[k], own)
+            block[g] = own
     return blocks
 
 
@@ -62,7 +91,7 @@
     for f in range(fronts):
         for r in range(steps):
             for c in range(steps):
-                work[f, r * NB : (r + 1) * NB, c * NB : (c + 1) * NB] = pivot_ref[(f * steps + r) * steps + c]
+                work[f, r * NB : (r + 1) * NB, c * NB : (c + 1) * NB] = pivot_ref[c, r, f]
     lane = lax.broadcasted_iota(jnp.int32, (NB, NB), 1)
     sub = lax.broadcasted_iota(jnp.int32, (NB, NB), 0)
     factor_ref[...] = jnp.zeros_like(factor_ref)
@@ -181,14 +210,14 @@
 def solve_border(where, columns, inv_hi, inv_lo, tile=512):
     fronts, size, _ = inv_hi.shape
     steps = size // NB
-    rows = columns.shape[1]
+    rows = columns.shape[2]
     inv_spec = pl.BlockSpec((1, NB, size), lambda i, w: (w[0], w[1], 0))
     return pl.pallas_call(
         border_kernel,
         grid_spec=pltpu.PrefetchScalarGridSpec(
             num_scalar_prefetch=1,
             grid=(rows // tile,),
-            in_specs=[pl.BlockSpec((steps, tile, NB), lambda i, w: (w[0], i, 0)), inv_spec, inv_spec],
+            in_specs=[pl.BlockSpec((steps, None, tile, NB), lambda i, w: (0, w[0], i, 0)), inv_spec, inv_spec],
             out_specs=pl.BlockSpec((tile, NB), lambda i, w: (i, 0)),
         ),
         out_shape=jax.ShapeDtypeStruct((rows, NB), F32),
@@ -200,10 +229,10 @@
 
 def product_kernel(hi_ref, lo_ref, columns_ref, out_ref):
     fronts = hi_ref.shape[0]
-    steps = columns_ref.shape[0] // fronts
+    steps = columns_ref.shape[0]
     total = None
     for f in range(fronts):
-        raw = jnp.concatenate([columns_ref[f * steps + k] for k in range(steps)], axis=1)
+        raw = jnp.concatenate([columns_ref[k, f] for k in range(steps)], axis=1)
         c_hi, c_lo = split(raw)
         part = dot3_nt(hi_ref[f], lo_ref[f], c_hi, c_lo)
         total = part if total is None else total + part
@@ -212,12 +241,12 @@
 
 def product(rows_hi, rows_lo, columns, tile=256):
     fronts, per, size = rows_hi.shape
-    blocks, width, _ = columns.shape
+    blocks, _, width, _ = columns.shape
     rows_spec = pl.BlockSpec((fronts, per, size), lambda i: (0, 0, 0), pipeline_mode=pl.Buffered(1))
     return pl.pallas_call(
         product_kernel,
         grid=(width // tile,),
-        in_specs=[rows_spec, rows_spec, pl.BlockSpec((blocks, tile, NB), lambda i: (0, i, 0))],
+        in_specs=[rows_spec, rows_spec, pl.BlockSpec((blocks, fronts, tile, NB), lambda i: (0, 0, i, 0))],
         out_specs=pl.BlockSpec((per, tile), lambda i: (0, i)),
         out_shape=jax.ShapeDtypeStruct((per, width), F32),
         compiler_params=pltpu.CompilerParams(vmem_limit_bytes=60 << 20),
@@ -282,9 +311,11 @@
     def exchange(x):
         return lax.all_to_all(x, both, split_axis=0, concat_axis=0, tiled=True)
 
-    pivots = lax.all_gather(pivot_local, ("sub", "row", "col"), axis=0)
+    pivots = pivot_local
+    for axis in ("sub", "row", "col"):
+        pivots = lax.all_gather(pivots, axis, axis=0)
     columns = lax.ppermute(border_local, ("row", "col"), turn)
-    columns = lax.all_gather(columns, both, axis=0)
+    columns = lax.all_gather(lax.all_gather(columns, "sub", axis=0), "row", axis=0)
     slots = exchange((targets % per).reshape(groups, capacity)).reshape(-1)
     arrived_rows = exchange(border_local[:rows_kept][ordering].reshape(groups, capacity, NB)).reshape(rows_kept, NB)
     arrived = exchange(window_local[ordering].reshape(groups, capacity, width)).reshape(rows_kept, width)

time: 839 us -> 691 us (0.82)
  Pallas kernels: 248 us -> 162 us
  waiting for transfers between devices: 478 us -> 430 us
  starting transfers between devices: 57.4 us -> 34.3 us
    pallas_call x1, Pallas kernels: 176 us -> 89.3 us  [factor_fronts(): pl.pallas_call(factor_kernel, in_specs=[pl.BlockSpec(memory_space=pltpu.S...]
    all_gather x2 -> x4, waiting for transfers between devices: 453 us -> 395 us  [the longest x1 337 us: per_device(): lax.all_gather(lax.all_gather(columns, 'sub', axis=0), 'row', axis=0)]
    all_to_all x3, starting transfers between devices: 53.5 us -> 27.8 us  [exchange(): return lax.all_to_all(x, both, split_axis=0, concat_axis=0, tiled=True)]
  transfers between devices with their start and end apart: 8 -> 10, of which waited for: 5 -> 7; matrix products, arithmetic and copies ran while one was open for 4% -> 5% of each run, Pallas kernels for 30% -> 24%
where the time goes in v2:
time: 691 us; the launch traced here: 684 us
  waiting for transfers between devices  430 us (62%)
  Pallas kernels  162 us (23%)
  starting transfers between devices  34.3 us (5%)
  local copies, waits for them, and re-layouts  25.4 us (4%)
  between operations  13.8 us (2%)
  other arithmetic  11.5 us (2%)
    all_gather x1, waiting for transfers between devices, per_device(): lax.all_gather(lax.all_gather(columns, 'sub', axis=0), 'row', axis=0)  337 us
    pallas_call x1, Pallas kernels, factor_fronts(): pl.pallas_call(factor_kernel, in_specs=[pl.BlockSpec(memory_space=pltpu.S...  89.3 us
    all_gather x2, waiting for transfers between devices, per_device(): pivots = lax.all_gather(pivots, axis, axis=0)  57.8 us
    all_to_all x3, starting transfers between devices, exchange(): return lax.all_to_all(x, both, split_axis=0, concat_axis=0, tiled=True)  27.8 us
    pallas_call x1, Pallas kernels, assemble(): pl.pallas_call(assemble_kernel, grid_spec=pltpu.PrefetchScalarGridSpec(nu...  26.5 us
    pallas_call x1, Pallas kernels, product(): pl.pallas_call(product_kernel, grid=(width // tile,), in_specs=[rows_spec...  22.1 us
    ppermute x1, waiting for transfers between devices, per_device(): columns = lax.ppermute(border_local, ('row', 'col'), turn)  21.7 us
    pallas_call x1, Pallas kernels, solve_both(): pl.pallas_call(rows_kernel, grid=(fronts, per // tile), in_specs=[pl.Bloc...  15.9 us
  transfers between devices with their start and end apart: 10, of which 7 were waited for; matrix products, arithmetic and copies ran while one was open for 5% of the time, Pallas kernels for 24%

profile of v2, /device:TPU:2, one launch (start us, length us, event | category | flops | bytes accessed | tf_op | source)
XLA Modules:
  0.0 683.6 jit_solution(5603310691945365519)
XLA Ops:
  7.2 0.0 all-gather.11.cloned.1.call-start
  7.2 6.8 all_gather.33
  14.0 0.0 all-gather.11.cloned.1.call-update
  14.0 0.0 all-gather.15.cloned.1.call-start
  14.1 1.9 collective-permute-start
  16.0 21.7 %collective-permute-done = f32[2048,128]{1,0:T(8,128)S(1)} collective-permute-done((f32[2048,128]{1,0:T(8,128)}, f32[2048,128]{1,0:T(8,128)S(1)}, u32[]{:S(2)}, u32[]{:S(2)}) %collective-permute-start) | collective-permute-done | bytes 1048608 | tf_op jit(solution)/shard_map/ppermute | solution.py:317
  37.7 0.0 copy-start
  37.7 1.0 copy-done
  38.7 0.0 all-gather.15.cloned.1.call-update
  38.7 0.0 all-gather.13.cloned.1.call-start
  38.8 27.8 %all-gather.11.cloned.1.call-done = f32[16,128,128]{2,1,0:T(8,128)} async-done(((f32[2,128,128]{2,1,0:T(8,128)}), f32[16,128,128]{2,1,0:T(8,128)}) %all-gather.11.cloned.1.call-update) | async-done | bytes 1048592 | tf_op jit(solution)/shard_map/all_gather | solution.py:316
  66.6 0.0 all-gather.13.cloned.1.call-update
  66.6 0.7 reduce
  67.4 4.4 sort.30
  71.8 0.7 all_to_all.12
  72.5 15.9 %all-to-all-start = ((s32[16,1,80]{2,1,0:T(1,128)}), s32[16,1,80]{2,1,0:T(1,128)S(1)}, u32[]{:S(2)}, u32[]{:S(2)}) async-start(s32[16,1,80]{2,1,0:T(1,128)} %all_to_all.12), calls=%async_computation | async-start | bytes 16384 | tf_op jit(solution)/shard_map/all_to_all | solution.py:312
  88.4 1.2 slice_bitcast_fusion
  89.6 3.2 gather_fusion.1
  92.7 1.8 all-to-all-done
  94.5 5.4 all-to-all-start.2
  100.0 0.0 all-gather.19.cloned.1.call-start
  100.0 0.5 broadcast.24
  100.5 0.7 reduce.4
  101.2 0.1 reshape.27
  101.3 5.0 sort.31
  106.3 0.0 copy-start.1
  106.3 11.0 %all-to-all-done.2 = f32[16,80,128]{2,1,0:T(8,128)S(1)} async-done(((f32[16,80,128]{2,1,0:T(8,128)}), f32[16,80,128]{2,1,0:T(8,128)S(1)}, u32[]{:S(2)}, u32[]{:S(2)}) %all-to-all-start.2) | async-done | bytes 655392 | tf_op jit(solution)/shard_map/all_to_all | solution.py:312
  117.3 3.1 gather_fusion.2
  120.5 0.0 all-gather.19.cloned.1.call-update
  120.5 0.0 all-gather.17.cloned.1.call-start
  120.5 0.6 all-gather.15.cloned.1.call-done
  121.2 0.0 all-gather.17.cloned.1.call-update
  121.2 14.7 %gather_fusion = f32[1280,2048]{1,0:T(8,128)} fusion(f32[1280,2048]{1,0:T(8,128)} %bitcast.18, s32[2048]{0:T(1024)S(1)} %pad_clamp_fusion.1), kind=kCustom, calls=%fused_computation | custom fusion | bytes 20976640 | tf_op jit(solution)/shard_map/gather | solution.py:321
  135.9 0.0 copy-done.1
  135.9 6.5 all-to-all-start.1
  142.4 0.6 pad_add_fusion.where_ref
  143.0 29.9 %all-gather.13.cloned.1.call-done = f32[64,2,128,128]{3,2,1,0:T(8,128)} async-done(((f32[8,2,128,128]{3,2,1,0:T(8,128)}), f32[64,2,128,128]{3,2,1,0:T(8,128)}) %all-gather.13.cloned.1.call-update) | async-done | bytes 8388624 | tf_op jit(solution)/shard_map/all_gather | solution.py:316
  172.9 89.3 %factor_fronts.1 = (bf16[2,1024,1024]{2,1,0:T(8,128)(2,1)}, bf16[2,1024,1024]{2,1,0:T(8,128)(2,1)}, f32[128,128]{1,0:T(8,128)}) custom-call(s32[3]{0:T(128)} %pad_add_fusion.where_ref, f32[8,8,2,128,128]{4,3,2,1,0:T(8,128)} %bitcast.27), custom_call_target="tpu_custom_call" | custom-call | flops 20000000000 | bytes 16777216 | tf_op jit(solution)/shard_map/factor_fronts/pallas_call | solution.py:152
  262.2 0.0 all-gather.19.cloned.1.call-done
  262.2 15.9 %solve_both.1 = (bf16[2,640,1024]{2,1,0:T(8,128)(2,1)}, bf16[2,640,1024]{2,1,0:T(8,128)(2,1)}) custom-call(f32[8,1280,128]{2,1,0:T(8,128)} %bitcast.28, bf16[2,1024,1024]{2,1,0:T(8,128)(2,1)} %get-tuple-element.12.hi_ref.inv_hi_ref, bf16[2,1024,1024]{2,1,0:T(8,128)(2,1)} %get-tuple-element.13.lo_ref.inv_lo_ref), custom_call_target="tpu_custom_call" | custom-call | flops 12000000000 | bytes 18874368 | tf_op jit(solution)/shard_map/solve_both/pallas_call | solution.py:193
  278.2 336.9 %all-gather.17.cloned.1.call-done = f32[16,2048,128]{2,1,0:T(8,128)} async-done(((f32[2,2048,128]{2,1,0:T(8,128)}), f32[16,2048,128]{2,1,0:T(8,128)}) %all-gather.17.cloned.1.call-update) | async-done | bytes 16777232 | tf_op jit(solution)/shard_map/all_gather | solution.py:318
  615.1 7.9 %solve_border.1 = f32[2048,128]{1,0:T(8,128)} custom-call(s32[3]{0:T(128)} %pad_add_fusion.where_ref, f32[8,2,2048,128]{3,2,1,0:T(8,128)} %bitcast.21, bf16[2,1024,1024]{2,1,0:T(8,128)(2,1)} %get-tuple-element.12.hi_ref.inv_hi_ref, bf16[2,1024,1024]{2,1,0:T(8,128)(2,1)} %get-tuple-element.13.lo_ref.inv_lo_ref), custom_call_target="tpu_custom_call" | custom-call | flops 1600000000 | bytes 10485760 | tf_op jit(solution)/shard_map/solve_border/pallas_call | solution.py:215
  623.0 4.4 collective-permute-start.1
  627.4 22.1 %product.1.product_ref = f32[640,2048]{1,0:T(8,128)} custom-call(bf16[2,640,1024]{2,1,0:T(8,128)(2,1)} %get-tuple-element.17.hi_ref, bf16[2,640,1024]{2,1,0:T(8,128)(2,1)} %get-tuple-element.18.lo_ref, f32[8,2,2048,128]{3,2,1,0:T(8,128)} %bitcast.22), custom_call_target="tpu_custom_call" | custom-call | flops 16000000000 | bytes 28311552 | tf_op jit(solution)/shard_map/product/pallas_call | solution.py:246
  649.5 0.0 all-to-all-done.1
  649.5 26.5 %assemble.1 = f32[640,2048]{1,0:T(8,128)} custom-call(s32[1280]{0:T(1024)} %copy-done.1, f32[1280,2048]{1,0:T(8,128)} %bitcast.12.arrived_ref, f32[640,2048]{1,0:T(8,128)} %product.1.product_ref), custom_call_target="tpu_custom_call" | custom-call | flops 4000000 | bytes 22020096 | tf_op jit(solution)/shard_map/assemble/pallas_call | solution.py:277
  676.1 0.0 collective-permute-done.1
  676.1 1.0 copy.8
  (8 shorter events, 0.1 us)
Async XLA Ops:
  7.2 59.5 %all-gather.11.cloned.1.call-start = ((), (), s32[]{:S(2)}) async-start(), calls=%async_computation.3 | async-start | bytes 1179648 | tf_op jit(solution)/shard_map/all_gather | solution.py:316
  14.0 107.1 %all-gather.15.cloned.1.call-start = ((), (), s32[]{:S(2)}) async-start(), calls=%async_computation.5 | async-start | bytes 3145728 | tf_op jit(solution)/shard_map/all_gather | solution.py:318
  14.1 23.7 %collective-permute-start = (f32[2048,128]{1,0:T(8,128)}, f32[2048,128]{1,0:T(8,128)S(1)}, u32[]{:S(2)}, u32[]{:S(2)}) collective-permute-start(f32[2048,128]{1,0:T(8,128)} %bitcast.26), channel_id=1, source_target_pairs={{0,0},{1,8},{2,16},{3,24},{4,32},{5,40},{6,48},{7,56},{8,1},{9,9},... | collective-permute-start | bytes 3145736 | tf_op jit(solution)/shard_map/ppermute | solution.py:317
  37.7 1.0 copy-start
  38.7 134.2 %all-gather.13.cloned.1.call-start = ((), (), s32[]{:S(2)}) async-start(), calls=%async_computation.4 | async-start | bytes 9437184 | tf_op jit(solution)/shard_map/all_gather | solution.py:316
  72.5 22.0 %all-to-all-start = ((s32[16,1,80]{2,1,0:T(1,128)}), s32[16,1,80]{2,1,0:T(1,128)S(1)}, u32[]{:S(2)}, u32[]{:S(2)}) async-start(s32[16,1,80]{2,1,0:T(1,128)} %all_to_all.12), calls=%async_computation | async-start | bytes 16384 | tf_op jit(solution)/shard_map/all_to_all | solution.py:312
  94.5 22.8 %all-to-all-start.2 = ((f32[16,80,128]{2,1,0:T(8,128)}), f32[16,80,128]{2,1,0:T(8,128)S(1)}, u32[]{:S(2)}, u32[]{:S(2)}) async-start(f32[16,80,128]{2,1,0:T(8,128)} %bitcast.14), calls=%async_computation.2 | async-start | bytes 1310720 | tf_op jit(solution)/shard_map/all_to_all | solution.py:312
  100.0 162.3 %all-gather.19.cloned.1.call-start = ((), (), s32[]{:S(2)}) async-start(), calls=%async_computation.7 | async-start | bytes 5898240 | tf_op jit(solution)/shard_map/all_gather | solution.py:324
  106.3 29.6 %copy-start.1 = (s32[1280]{0:T(1024)}, s32[1280]{0:T(1024)S(1)}, u32[]{:S(2)}) copy-start(s32[1280]{0:T(1024)S(1)} %get-tuple-element.15.place_ref) | copy-start | bytes 15364
  120.5 494.6 %all-gather.17.cloned.1.call-start = ((), (), s32[]{:S(2)}) async-start(), calls=%async_computation.6 | async-start | bytes 18874368 | tf_op jit(solution)/shard_map/all_gather | solution.py:318
  135.9 513.6 %all-to-all-start.1 = ((f32[16,80,2048]{2,1,0:T(8,128)}), f32[16,80,2048]{2,1,0:T(8,128)}, u32[]{:S(2)}, u32[]{:S(2)}) async-start(f32[16,80,2048]{2,1,0:T(8,128)} %bitcast.20), calls=%async_computation.1 | async-start | bytes 20971520 | tf_op jit(solution)/shard_map/all_to_all | solution.py:312
  623.0 53.0 %collective-permute-start.1 = (f32[2048,128]{1,0:T(8,128)}, f32[2048,128]{1,0:T(8,128)S(1)}, u32[]{:S(2)}, u32[]{:S(2)}) collective-permute-start(f32[2048,128]{1,0:T(8,128)} %solve_border.1), channel_id=1, source_target_pairs={{0,0},{1,8},{2,16},{3,24},{4,32},{5,40},{6,48},{7,56},{8,1},{9,9},... | collective-permute-start | bytes 3145736 | tf_op jit(solution)/shard_map/ppermute | solution.py:329
Sparse Core Ops, SparseCore 0:
  14.1 52.4 all-gather.10
  68.8 52.2 all-gather.14
  122.9 50.0 all-gather.12
  174.5 36.6 all-gather.18
  212.6 402.4 all-gather.16
